TPU v7x, 32 devices: a whole 2x2x4 slice. The times are simulated.
32 devices in a mesh: dp: 4 (over y, x), seq: 4 (over z), feat: 2 (over core).
Axes of the slice: x: 2, y: 2, z: 4, core: 2. Of those that a mesh axis runs over, the one named last changes fastest.
Arguments:
- tokens: bfloat16 [16384, 2048], P(('dp', 'seq')), parts along dimension 0, may hold values from -6 to 6
- w_query: bfloat16 [2048, 256], P(None, 'feat'), may hold values from -0.125 to 0.125
- w_key: bfloat16 [2048, 256], P(None, 'feat'), may hold values from -0.125 to 0.125
- value_weight: bfloat16 [2048, 2048], P(None, 'feat'), may hold values from -0.125 to 0.125
- w_out: bfloat16 [2048, 2048], P(None, 'feat'), may hold values from -0.125 to 0.125
Outputs:
- mixed: bfloat16 [16384, 2048], P(('dp', 'seq'), 'feat'), parts along dimension 0
There are 4 independent parts, one for each index of `dp`. A program takes and returns all parts, laid end to end along the dimension named above; an argument that names none is the same for every part. Nothing has to cross between parts.
All inputs are finite; a program needn't handle non-finite values.
Results may differ from a plain program's by a relative error of at most 0.009.
Values may be sent and summed in bfloat16 or wider, within the bound.
No kernel may reach another device: no remote copies, remote signals or barrier semaphores. Data moves between devices by JAX's collectives and lax.ppermute only.
A program may use at most 64 MiB of HBM per device.

v0:
```python
import jax
import jax.numpy as jnp
from jax import lax
from jax.sharding import PartitionSpec as P

DK = 16
DV = 128


def key_features(key_rows):
    as_float = key_rows.astype(jnp.float32)
    row_count = key_rows.shape[0]
    head_total = key_rows.shape[1]
    linear = jnp.transpose(as_float, (1, 2, 0))
    square = jnp.einsum("nha,nhb->habn", as_float, as_float).reshape(head_total, -1, row_count)
    ones_row = jnp.ones((head_total, 1, row_count), jnp.float32)
    return jnp.concatenate([ones_row, linear, square], axis=1).astype(jnp.bfloat16)


def query_features(query_rows):
    as_float = query_rows.astype(jnp.float32)
    row_count = query_rows.shape[0]
    head_total = query_rows.shape[1]
    linear = jnp.transpose(as_float, (1, 2, 0)) * 0.25
    square = jnp.einsum("nha,nhb->habn", as_float, as_float).reshape(head_total, -1, row_count) * (
        1.0 / 32.0
    )
    ones_row = jnp.ones((head_total, 1, row_count), jnp.float32)
    return jnp.concatenate([ones_row, linear, square], axis=1)


def local(tokens, w_query, w_key, value_weight, w_out):
    row_count = tokens.shape[0]
    local_heads = value_weight.shape[1] // DV
    query_rows = (
        jnp.dot(tokens, w_query, preferred_element_type=jnp.float32)
        .astype(jnp.bfloat16)
        .reshape(row_count, local_heads, DK)
    )
    key_rows = (
        jnp.dot(tokens, w_key, preferred_element_type=jnp.float32)
        .astype(jnp.bfloat16)
        .reshape(row_count, local_heads, DK)
    )
    value_matrix = (
        jnp.dot(tokens, value_weight, preferred_element_type=jnp.float32)
        .astype(jnp.bfloat16)
        .reshape(row_count, local_heads, DV)
    )
    block_state = jnp.einsum(
        "hfn,nhd->hfd", key_features(key_rows), value_matrix, preferred_element_type=jnp.float32
    )
    zero_state = jnp.zeros(block_state.shape, jnp.float32)
    my_block = lax.axis_index("seq")
    piece = lax.all_gather(
        block_state[None].astype(jnp.bfloat16), "seq", axis=0, tiled=True
    ).astype(jnp.float32)
    order = lax.broadcasted_iota(jnp.int32, (piece.shape[0],), 0)
    keep = (order < my_block).astype(jnp.float32)
    earlier = zero_state + jnp.sum(piece * keep[:, None, None, None], axis=0)
    scores = (
        jnp.einsum("nha,mha->hnm", query_rows, key_rows, preferred_element_type=jnp.float32) * 0.25
    )
    causal = lax.broadcasted_iota(jnp.int32, (row_count, row_count), 0) >= lax.broadcasted_iota(
        jnp.int32, (row_count, row_count), 1
    )
    weight_tensors = jnp.where(causal[None], 1.0 + scores + 0.5 * scores * scores, 0.0).astype(
        jnp.bfloat16
    )
    local_portion = jnp.einsum(
        "iot,tiw->oiw", weight_tensors, value_matrix, preferred_element_type=jnp.float32
    )
    carried = jnp.einsum(
        "hfn,hfd->nhd", query_features(query_rows), earlier, precision=lax.Precision.HIGHEST
    )
    numerator = carried + local_portion
    scale = lax.rsqrt(jnp.mean(numerator * numerator, axis=-1, keepdims=True) + 1e-06)
    normalized_rows = (numerator * scale).reshape(row_count, local_heads * DV).astype(jnp.bfloat16)
    mixed = jnp.dot(
        lax.all_gather(normalized_rows, "feat", axis=1, tiled=True),
        w_out,
        preferred_element_type=jnp.float32,
    )
    return mixed.astype(jnp.bfloat16)


def solution(mesh):
    placed = (
        P(("dp", "seq"), None),
        P(None, "feat"),
        P(None, "feat"),
        P(None, "feat"),
        P(None, "feat"),
    )
    return jax.shard_map(
        local, mesh=mesh, in_specs=placed, out_specs=P(("dp", "seq"), "feat"), check_vma=False
    )
```

profile of v0, /device:TPU:0, one launch (start us, length us, event | category | flops | bytes accessed | tf_op | source)
XLA Modules:
  0.0 135.8 jit_solution(15695235256979759861)
XLA Ops:
  6.5 0.0 all-gather.6.cloned.1.call-start
  6.5 1.0 copy-done
  7.6 3.9 %convolution_convert_fusion.3 = bf16[1024,128]{0,1:T(8,128)(2,1)S(1)} fusion(bf16[1024,2048]{1,0:T(8,128)(2,1)} %param.5, bf16[2048,128]{1,0:T(8,128)(2,1)S(1)} %copy-done), kind=kOutput, calls=%fused_computation.30 | convolution fusion | flops 537001984 | bytes 4980736 | tf_op jit(solution)/shard_map/dot_general | solution.py:41
  11.4 0.0 copy-start.1
  11.5 1.3 multiply_convert_fusion
  12.8 0.8 copy-done.1
  13.6 4.8 %convolution_convert_fusion.1 = bf16[1024,1024]{0,1:T(8,128)(2,1)S(1)} fusion(bf16[1024,2048]{1,0:T(8,128)(2,1)S(1)} %copy-done.1, bf16[2048,1024]{1,0:T(8,128)(2,1)S(1)} %copy-done.3), kind=kOutput, calls=%fused_computation.27 | convolution fusion | flops 4296015872 | bytes 10485760 | tf_op jit(solution)/shard_map/dot_general | solution.py:46
  18.5 0.0 copy-start.4
  18.5 0.0 copy-start.2
  18.5 1.7 %fusion.20 = bf16[8,273,128]{2,1,0:T(8,128)(2,1)S(1)} fusion(bf16[1024,8,128]{0,2,1:T(8,128)(2,1)S(1)} %bitcast.51, bf16[8,256,1024]{2,1,0:T(8,128)(2,1)S(1)} %bitcast.47, bf16[8,16,1024]{2,1,0:T(8,128)(2,1)S(1)} %bitcast.49, bf16[273]{0:T(512)(128)(2,1)S(1)} %pad.3.clone), kind=kOutput, calls=%fused_computation.28 | convolution fusion | flops 586220544 | bytes 7113250 | tf_op jit(solution)/shard_map/hfn,nhd->hfd/dot_general | solution.py:50
  20.2 0.9 copy.10
  21.1 0.0 all-gather.6.cloned.1.call-update
  21.1 0.0 all-gather.4.cloned.1.call-start
  21.2 0.3 iota_compare_fusion
  21.5 3.7 %convolution_convert_fusion.2 = bf16[1024,128]{0,1:T(8,128)(2,1)S(1)} fusion(bf16[1024,2048]{1,0:T(8,128)(2,1)} %param.5, bf16[2048,128]{1,0:T(8,128)(2,1)S(1)} %copy-done.2), kind=kOutput, calls=%fused_computation.29 | convolution fusion | flops 537001984 | bytes 4980736 | tf_op jit(solution)/shard_map/dot_general | solution.py:36
  25.3 4.4 %multiply_multiply_fusion = f32[8,1024,16,16]{1,2,3,0:T(8,128)} fusion(f32[8,1024,16]{1,2,0:T(8,128)S(1)} %convert_bitcast_fusion), kind=kLoop, calls=%fused_computation.8 | loop fusion | flops 4194304 | bytes 8912896 | tf_op jit(solution)/shard_map/mul | solution.py:25
  29.8 42.7 %all-gather.6.cloned.1.call-done = bf16[32,273,128]{2,0,1:T(8,128)(2,1)} async-done(((bf16[8,273,128]{2,0,1:T(8,128)(2,1)}), bf16[32,273,128]{2,0,1:T(8,128)(2,1)}) %all-gather.6.cloned.1.call-update) | async-done | bytes 2236432 | tf_op jit(solution)/shard_map/all_gather | solution.py:55
  72.5 2.8 %fusion.13 = f32[8,273,128]{2,0,1:T(8,128)S(1)} fusion(bf16[32,273,128]{2,0,1:T(8,128)(2,1)} %all-gather.6.cloned.1.call-done, f32[4]{0:T(128)S(1)} %compare_convert_fusion), kind=kLoop, calls=%fused_computation.17 | loop fusion | flops 3075072 | bytes 3354640 | tf_op jit(solution)/shard_map/reduce_sum | solution.py:60
  75.4 12.1 %fusion.2 = f32[8,128,1024]{2,1,0:T(8,128)} fusion(f32[8,256,1024]{2,1,0:T(8,128)} %bitcast.45, f32[8,16,1024]{2,1,0:T(8,128)S(1)} %fusion.24, f32[273]{0:T(512)S(1)} %pad.clone, f32[8,273,128]{2,0,1:T(8,128)S(1)} %fusion.13), kind=kOutput, calls=%fused_computation.3 | convolution fusion | flops 3439607808 | bytes 14226500 | tf_op jit(solution)/shard_map/hfn,hfd->nhd/dot_general | solution.py:73
  87.4 16.0 %fusion.14 = (f32[1024,8]{0,1:T(8,128)S(1)}, f32[8,128,1024]{2,1,0:T(8,128)}) fusion(f32[8,128,1024]{2,1,0:T(8,128)} %fusion.2, bf16[1024,8,128]{0,2,1:T(8,128)(2,1)} %bitcast.52, pred[1024,1024]{1,0:T(8,128)(4,1)S(1)} %iota_compare_fusion, bf16[1024,8,16]{0,2,1:T(8,128)(2,1)S(1)} %bitcast.48, bf16[1024,8,16]{0,2,1:T(8,128)(2,1)S(1)} %bitcast.50), kind=kOutput, calls=%fused_computation.20 | convolution fusion | flops 2477776896 | bytes 12091392 | tf_op jit(solution)/shard_map/iot,tiw->oiw/dot_general | solution.py:70
  103.4 4.1 %fusion.15 = bf16[1024,8,128]{0,2,1:T(8,128)(2,1)} fusion(f32[8,128,1024]{2,1,0:T(8,128)} %get-tuple-element.6, f32[1024,8]{0,1:T(8,128)S(1)} %add_rsqrt_fusion), kind=kLoop, calls=%fused_computation.21 | loop fusion | flops 2097152 | bytes 6324224 | tf_op jit(solution)/shard_map/convert_element_type | solution.py:78
  107.5 0.0 all-gather.4.cloned.1.call-update
  107.6 12.0 %all-gather.4.cloned.1.call-done = bf16[1024,2048]{0,1:T(8,128)(2,1)} async-done(((bf16[1024,1024]{0,1:T(8,128)(2,1)}), bf16[1024,2048]{0,1:T(8,128)(2,1)}) %all-gather.4.cloned.1.call-update) | async-done | bytes 4194320 | tf_op jit(solution)/shard_map/all_gather | solution.py:80
  119.6 9.4 %convolution_convert_fusion = bf16[1024,1024]{1,0:T(8,128)(2,1)} fusion(bf16[1024,2048]{0,1:T(8,128)(2,1)} %all-gather.4.cloned.1.call-done, bf16[2048,1024]{1,0:T(8,128)(2,1)} %param.9), kind=kOutput, calls=%fused_computation.26 | convolution fusion | flops 4296015872 | bytes 10485760 | tf_op jit(solution)/shard_map/dot_general | solution.py:79
  (12 shorter events, 0.2 us)
Async XLA Ops:
  6.5 1.0 copy-start
  6.5 66.0 %all-gather.6.cloned.1.call-start = ((), (), s32[]{:S(2)}) async-start(), calls=%async_computation.1 | async-start | bytes 2795520 | tf_op jit(solution)/shard_map/all_gather | solution.py:55
  7.6 5.2 %copy-start.3 = (bf16[2048,1024]{1,0:T(8,128)(2,1)S(1)}, bf16[2048,1024]{1,0:T(8,128)(2,1)}, u32[]{:S(2)}) copy-start(bf16[2048,1024]{1,0:T(8,128)(2,1)} %param.8) | copy-start | bytes 12582916
  11.4 2.2 %copy-start.1 = (bf16[1024,2048]{1,0:T(8,128)(2,1)S(1)}, bf16[1024,2048]{1,0:T(8,128)(2,1)}, u32[]{:S(2)}) copy-start(bf16[1024,2048]{1,0:T(8,128)(2,1)} %param.5) | copy-start | bytes 12582916
  18.5 1.7 %copy-start.4 = (bf16[1024,1024]{0,1:T(8,128)(2,1)}, bf16[1024,1024]{0,1:T(8,128)(2,1)S(1)}, u32[]{:S(2)}) copy-start(bf16[1024,1024]{0,1:T(8,128)(2,1)S(1)} %convolution_convert_fusion.1) | copy-start | bytes 6291460
  18.5 3.0 %copy-start.2 = (bf16[2048,128]{1,0:T(8,128)(2,1)S(1)}, bf16[2048,128]{1,0:T(8,128)(2,1)}, u32[]{:S(2)}) copy-start(bf16[2048,128]{1,0:T(8,128)(2,1)} %param.6) | copy-start | bytes 1572868
  21.1 98.4 %all-gather.4.cloned.1.call-start = ((), (), s32[]{:S(2)}) async-start(), calls=%async_computation | async-start | bytes 6291456 | tf_op jit(solution)/shard_map/all_gather | solution.py:80
Sparse Core Ops, SparseCore 0:
  21.2 51.2 all-gather.5
  107.7 11.8 all-gather.3
where the time goes:
time: 136 us
  waiting for transfers between devices  54.8 us (40%)
  matrix products  51.5 us (38%)
  between operations  13.6 us (10%)
  other arithmetic  13.1 us (10%)
  local copies, waits for them, and re-layouts  2.79 us (2%)
    all_gather x1, waiting for transfers between devices, local(): lax.all_gather(block_state[None].astype(jnp.bfloat16), 'seq', axis=0, til...  42.7 us
    dot_general x1, matrix products, local(): jnp.einsum('iot,tiw->oiw', weight_tensors, value_matrix, preferred_elemen...  16 us
    dot_general x1, matrix products, local(): jnp.einsum('hfn,hfd->nhd', query_features(query_rows), earlier, precision...  12.1 us
    all_gather x1, waiting for transfers between devices, local(): lax.all_gather(normalized_rows, 'feat', axis=1, tiled=True)  12 us
    dot_general x1, matrix products, local(): jnp.dot(lax.all_gather(normalized_rows, 'feat', axis=1, tiled=True), w_ou...  9.36 us
    dot_general x1, matrix products, local(): jnp.dot(tokens, value_weight, preferred_element_type=jnp.float32)  4.81 us
    mul x1, other arithmetic, query_features(): jnp.einsum('nha,nhb->habn', as_float, as_float)  4.45 us
    convert_element_type x1, other arithmetic, local(): (numerator * scale).reshape(row_count, local_heads * DV)  4.11 us
  transfers between devices with their start and end apart: 2, of which 2 were waited for; matrix products, arithmetic and copies ran while one was open for 6% of the time, Pallas kernels for 0%

commit v1 on v0

--- a/solution.py
+++ b/solution.py
@@ -5,6 +5,27 @@
 
 DK = 16
 DV = 128
+
+
+def collect(array, axis, dim):
+    count, index, width = (lax.axis_size(axis), lax.axis_index(axis), array.shape[dim])
+    right = [(i, (i + 1) % count) for i in range(count)]
+    behind = [(i, (i - 1) % count) for i in range(count)]
+    filled = jnp.zeros((*array.shape[:dim], count * width, *array.shape[dim + 1 :]), array.dtype)
+    filled = lax.dynamic_update_slice_in_dim(filled, array, index * width, axis=dim)
+    from_left = from_right = array
+    half = count // 2
+    for lap in range(1, half + 1):
+        from_left = lax.ppermute(from_left, axis, right)
+        filled = lax.dynamic_update_slice_in_dim(
+            filled, from_left, (index - lap) % count * width, axis=dim
+        )
+        if lap < count - half:
+            from_right = lax.ppermute(from_right, axis, behind)
+            filled = lax.dynamic_update_slice_in_dim(
+                filled, from_right, (index + lap) % count * width, axis=dim
+            )
+    return filled
 
 
 def key_features(key_rows):
@@ -52,9 +73,7 @@
     )
     zero_state = jnp.zeros(block_state.shape, jnp.float32)
     my_block = lax.axis_index("seq")
-    piece = lax.all_gather(
-        block_state[None].astype(jnp.bfloat16), "seq", axis=0, tiled=True
-    ).astype(jnp.float32)
+    piece = collect(block_state[None].astype(jnp.bfloat16), "seq", 0).astype(jnp.float32)
     order = lax.broadcasted_iota(jnp.int32, (piece.shape[0],), 0)
     keep = (order < my_block).astype(jnp.float32)
     earlier = zero_state + jnp.sum(piece * keep[:, None, None, None], axis=0)

time: 136 us -> 115 us (0.85)
  waiting for transfers between devices: 54.8 us -> 25.6 us
  starting transfers between devices: 0.04 us -> 5.36 us
  local copies, waits for them, and re-layouts: 2.79 us -> 6.73 us
  other arithmetic: 13.1 us -> 11.5 us
    all_gather x1 -> x0, waiting for transfers between devices: 42.7 us -> none  [local(): lax.all_gather(block_state[None].astype(jnp.bfloat16), 'seq', axis=0, til...]
    ppermute x0 -> x3, waiting for transfers between devices: none -> 13.6 us  [the longest x2 13.6 us: collect(): from_left = lax.ppermute(from_left, axis, right)]
    ppermute x0 -> x3, starting transfers between devices: none -> 5.36 us  [the longest x2 3.34 us: collect(): from_left = lax.ppermute(from_left, axis, right)]
    dynamic_update_slice x0 -> x3, local copies, waits for them, and re-layouts: none -> 3.76 us  [the longest x2 2.52 us: collect(): lax.dynamic_update_slice_in_dim(filled, from_left, (index - lap) % count...]
    dot_general x1, matrix products: 1.7 us -> 4.85 us  [local(): jnp.einsum('hfn,nhd->hfd', key_features(key_rows), value_matrix, preferre...]
    reduce_sum x1, other arithmetic: 2.85 us -> 0.53 us  [local(): earlier = zero_state + jnp.sum(piece * keep[:, None, None, None], axis=0)]
    dot_general x1, matrix products: 3.7 us -> 1.51 us  [local(): jnp.dot(tokens, w_query, preferred_element_type=jnp.float32)]
    convert_element_type x1, other arithmetic: 4.11 us -> 1.96 us  [local(): (numerator * scale).reshape(row_count, local_heads * DV)]
  transfers between devices with their start and end apart: 2 -> 4, of which waited for: 2 -> 2; matrix products, arithmetic and copies ran while one was open for 6% -> 22% of each run, Pallas kernels for 0% -> 0%
where the time goes in v1:
time: 115 us; the launch traced here: 114 us
  matrix products  51.4 us (45%)
  waiting for transfers between devices  25.6 us (22%)
  between operations  13.6 us (12%)
  other arithmetic  11.5 us (10%)
  local copies, waits for them, and re-layouts  6.73 us (6%)
  starting transfers between devices  5.36 us (5%)
    dot_general x1, matrix products, local(): jnp.einsum('iot,tiw->oiw', weight_tensors, value_matrix, preferred_elemen...  15.3 us
    ppermute x2, waiting for transfers between devices, collect(): from_left = lax.ppermute(from_left, axis, right)  13.6 us
    all_gather x1, waiting for transfers between devices, local(): lax.all_gather(normalized_rows, 'feat', axis=1, tiled=True)  12 us
    dot_general x1, matrix products, local(): jnp.einsum('hfn,hfd->nhd', query_features(query_rows), earlier, precision...  10.7 us
    dot_general x1, matrix products, local(): jnp.dot(lax.all_gather(normalized_rows, 'feat', axis=1, tiled=True), w_ou...  9.36 us
    dot_general x1, matrix products, local(): jnp.dot(tokens, value_weight, preferred_element_type=jnp.float32)  5.78 us
    dot_general x1, matrix products, local(): jnp.einsum('hfn,nhd->hfd', key_features(key_rows), value_matrix, preferre...  4.85 us
    mul x1, other arithmetic, query_features(): jnp.einsum('nha,nhb->habn', as_float, as_float)  4.44 us
  transfers between devices with their start and end apart: 4, of which 2 were waited for; matrix products, arithmetic and copies ran while one was open for 22% of the time, Pallas kernels for 0%

profile of v1, /device:TPU:0, one launch (start us, length us, event | category | flops | bytes accessed | tf_op | source)
XLA Modules:
  0.0 114.3 jit_solution(14940290484713164260)
XLA Ops:
  6.5 1.0 copy-done
  7.6 3.9 %convolution_convert_fusion.3 = bf16[1024,128]{0,1:T(8,128)(2,1)S(1)} fusion(bf16[1024,2048]{1,0:T(8,128)(2,1)} %param.5, bf16[2048,128]{1,0:T(8,128)(2,1)S(1)} %copy-done), kind=kOutput, calls=%fused_computation.29 | convolution fusion | flops 537001984 | bytes 4980736 | tf_op jit(solution)/shard_map/dot_general | solution.py:62
  11.5 3.2 %multiply_convert_fusion = bf16[8,1024,16,16]{1,2,3,0:T(8,128)(2,1)} fusion(f32[8,1024,16]{1,2,0:T(8,128)S(1)} %convert_bitcast_fusion.1), kind=kLoop, calls=%fused_computation.9 | loop fusion | flops 4194304 | bytes 4718592 | tf_op jit(solution)/shard_map/convert.13
  14.7 5.8 %convolution_convert_fusion.1 = bf16[1024,1024]{0,1:T(8,128)(2,1)} fusion(bf16[1024,2048]{1,0:T(8,128)(2,1)S(1)} %copy-done.1, bf16[2048,1024]{1,0:T(8,128)(2,1)S(1)} %copy-done.8), kind=kOutput, calls=%fused_computation.25 | convolution fusion | flops 4296015872 | bytes 10485760 | tf_op jit(solution)/shard_map/dot_general | solution.py:67
  20.5 0.3 broadcast_in_dim.19
  20.8 4.8 %constant_dynamic-update-slice_fusion = (bf16[4,8,273,128]{3,2,1,0:T(8,128)(2,1)S(1)}, bf16[1,8,273,128]{3,2,1,0:T(8,128)(2,1)S(1)}) fusion(bf16[4,8,273,128]{3,2,1,0:T(8,128)(2,1)S(1)} %broadcast_in_dim.19, s32[]{:T(128)S(6)} %select_n.31, bf16[1024,8,128]{0,2,1:T(8,128)(2,1)} %bitcast.51, bf16[8,256,1024]{2,1,0:T(8,128)(2,1)} %bitcast.44, ...), kind=kOutput, calls=%fused_computation.39 | convolution fusion | flops 586220544 | bytes 7701508 | tf_op jit(solution)/shard_map/hfn,nhd->hfd/dot_general | solution.py:71
  25.7 0.9 copy.8
  26.6 3.1 %collective-permute-start = (bf16[1,8,273,128]{3,1,2,0:T(8,128)(2,1)}, bf16[1,8,273,128]{3,1,2,0:T(8,128)(2,1)}, u32[]{:S(2)}, u32[]{:S(2)}) collective-permute-start(bf16[1,8,273,128]{3,1,2,0:T(8,128)(2,1)} %copy.8), channel_id=1, source_target_pairs={{0,2},{2,4},{4,6},{6,0},{1,3},{3,5},{5,7},{7,1},{8,10},{10,12},{12... | collective-permute-start | bytes 1677320 | tf_op jit(solution)/shard_map/ppermute | solution.py:19
  29.6 2.0 %collective-permute-start.1 = (bf16[1,8,273,128]{3,1,2,0:T(8,128)(2,1)}, bf16[1,8,273,128]{3,1,2,0:T(8,128)(2,1)}, u32[]{:S(2)}, u32[]{:S(2)}) collective-permute-start(bf16[1,8,273,128]{3,1,2,0:T(8,128)(2,1)} %copy.8), channel_id=1, source_target_pairs={{0,6},{2,0},{4,2},{6,4},{1,7},{3,1},{5,3},{7,5},{8,14},{10,8},{12,... | collective-permute-start | bytes 1677320 | tf_op jit(solution)/shard_map/ppermute | solution.py:24
  31.7 1.3 %iota_compare_fusion = pred[1024,1024]{1,0:T(8,128)(4,1)} fusion(), kind=kLoop, calls=%fused_computation.21 | loop fusion | flops 1048576 | bytes 1048576 | tf_op jit(solution)/shard_map/ge | solution.py:83
  33.0 1.5 %convolution_convert_fusion.2 = bf16[1024,128]{0,1:T(8,128)(2,1)S(1)} fusion(bf16[1024,2048]{1,0:T(8,128)(2,1)S(1)} %copy-done.2, bf16[2048,128]{1,0:T(8,128)(2,1)S(1)} %copy-done.7), kind=kOutput, calls=%fused_computation.28 | convolution fusion | flops 537001984 | bytes 4980736 | tf_op jit(solution)/shard_map/dot_general | solution.py:57
  34.5 0.7 copy-done.4
  35.2 15.3 %fusion = f32[8,128,1024]{2,1,0:T(8,128)} fusion(bf16[1024,8,128]{0,2,1:T(8,128)(2,1)} %bitcast.52, pred[1024,1024]{1,0:T(8,128)(4,1)} %iota_compare_fusion, bf16[1024,8,16]{0,2,1:T(8,128)(2,1)} %bitcast.46, bf16[1024,8,16]{0,2,1:T(8,128)(2,1)} %bitcast.50), kind=kOutput, calls=%fused_computation.1 | convolution fusion | flops 2474639360 | bytes 7864320 | tf_op jit(solution)/shard_map/iot,tiw->oiw/dot_general | solution.py:89
  50.6 4.4 %multiply_multiply_fusion = f32[8,1024,16,16]{1,2,3,0:T(8,128)} fusion(f32[8,1024,16]{1,2,0:T(8,128)S(1)} %convert_bitcast_fusion), kind=kLoop, calls=%fused_computation.8 | loop fusion | flops 4194304 | bytes 8912896 | tf_op jit(solution)/shard_map/mul | solution.py:46
  55.1 0.3 collective-permute-start.2
  55.4 1.3 %copy_dynamic-update-slice_fusion.2 = bf16[4,8,273,128]{3,2,1,0:T(8,128)(2,1)S(1)} fusion(bf16[4,8,273,128]{3,2,1,0:T(8,128)(2,1)S(1)} %get-tuple-element.5, s32[]{:T(128)S(6)} %select_n.33, bf16[1,8,273,128]{3,1,2,0:T(8,128)(2,1)} %collective-permute-done), kind=kLoop, calls=%fused_computation.34 | loop fusion | bytes 1132548 | tf_op jit(solution)/shard_map/dynamic_update_slice | solution.py:20
  56.8 1.2 %copy_dynamic-update-slice_fusion.1 = bf16[4,8,273,128]{3,2,1,0:T(8,128)(2,1)S(1)} fusion(bf16[4,8,273,128]{3,2,1,0:T(8,128)(2,1)S(1)} %copy_dynamic-update-slice_fusion.2, s32[]{:T(128)S(6)} %select_n.35, bf16[1,8,273,128]{3,1,2,0:T(8,128)(2,1)} %collective-permute-done.1), kind=kLoop, calls=%fused_computation.33 | loop fusion | bytes 1132548 | tf_op jit(solution)/shard_map/dynamic_update_slice | solution.py:25
  58.0 13.6 %collective-permute-done.2 = bf16[1,8,273,128]{3,1,2,0:T(8,128)(2,1)} collective-permute-done((bf16[1,8,273,128]{3,1,2,0:T(8,128)(2,1)}, bf16[1,8,273,128]{3,1,2,0:T(8,128)(2,1)}, u32[]{:S(2)}, u32[]{:S(2)}) %collective-permute-start.2) | collective-permute-done | bytes 559136 | tf_op jit(solution)/shard_map/ppermute | solution.py:19
  71.6 1.2 %copy_dynamic-update-slice_fusion = bf16[4,8,273,128]{3,2,1,0:T(8,128)(2,1)S(1)} fusion(bf16[4,8,273,128]{3,2,1,0:T(8,128)(2,1)S(1)} %copy_dynamic-update-slice_fusion.1, s32[]{:T(128)S(6)} %select_n.37, bf16[1,8,273,128]{3,1,2,0:T(8,128)(2,1)} %collective-permute-done.2), kind=kLoop, calls=%fused_computation.32 | loop fusion | bytes 1132548 | tf_op jit(solution)/shard_map/dynamic_update_slice | solution.py:20
  72.8 0.5 multiply_reduce_fusion
  73.3 10.7 %fusion.13 = (f32[1024,8]{0,1:T(8,128)S(1)}, f32[8,128,1024]{2,1,0:T(8,128)S(1)}) fusion(f32[8,128,1024]{2,1,0:T(8,128)S(1)} %copy-done.3, f32[8,273,128]{2,1,0:T(8,128)S(1)} %multiply_reduce_fusion, f32[8,256,1024]{2,1,0:T(8,128)} %bitcast.42, f32[8,16,1024]{2,1,0:T(8,128)S(1)} %fusion.25, f32[273]{0:T(512)S(1)} %pad.clone), kind=kOutput, calls=%fused_computation.19 | convolution fusion | flops 3442745344 | bytes 18453572 | tf_op jit(solution)/shard_map/hfn,hfd->nhd/dot_general | solution.py:92
  84.1 2.0 %fusion.14 = bf16[1024,8,128]{0,2,1:T(8,128)(2,1)} fusion(f32[8,128,1024]{2,1,0:T(8,128)S(1)} %get-tuple-element.8, f32[1024,8]{0,1:T(8,128)S(1)} %add_rsqrt_fusion), kind=kLoop, calls=%fused_computation.20 | loop fusion | flops 2097152 | bytes 6324224 | tf_op jit(solution)/shard_map/convert_element_type | solution.py:97
  86.1 12.0 %all-gather.2.cloned.1.call-done = bf16[1024,2048]{0,1:T(8,128)(2,1)} async-done(((bf16[1024,1024]{0,1:T(8,128)(2,1)}), bf16[1024,2048]{0,1:T(8,128)(2,1)}) %all-gather.2.cloned.1.call-update) | async-done | bytes 4194320 | tf_op jit(solution)/shard_map/all_gather | solution.py:99
  98.1 9.4 %convolution_convert_fusion = bf16[1024,1024]{1,0:T(8,128)(2,1)} fusion(bf16[1024,2048]{0,1:T(8,128)(2,1)} %all-gather.2.cloned.1.call-done, bf16[2048,1024]{1,0:T(8,128)(2,1)} %param.9), kind=kOutput, calls=%fused_computation.24 | convolution fusion | flops 4296015872 | bytes 10485760 | tf_op jit(solution)/shard_map/dot_general | solution.py:98
  (27 shorter events, 0.2 us)
Async XLA Ops:
  6.5 1.0 copy-start
  6.5 91.5 %all-gather.2.cloned.1.call-start = ((), (), s32[]{:S(2)}) async-start(), calls=%async_computation | async-start | bytes 6291456 | tf_op jit(solution)/shard_map/all_gather | solution.py:99
  7.6 7.1 %copy-start.8 = (bf16[2048,1024]{1,0:T(8,128)(2,1)S(1)}, bf16[2048,1024]{1,0:T(8,128)(2,1)}, u32[]{:S(2)}) copy-start(bf16[2048,1024]{1,0:T(8,128)(2,1)} %param.8) | copy-start | bytes 12582916
  11.4 9.4 %copy-start.6 = (bf16[1024,128]{0,1:T(8,128)(2,1)}, bf16[1024,128]{0,1:T(8,128)(2,1)S(1)}, u32[]{:S(2)}) copy-start(bf16[1024,128]{0,1:T(8,128)(2,1)S(1)} %convolution_convert_fusion.3) | copy-start | bytes 786436
  11.4 3.3 %copy-start.1 = (bf16[1024,2048]{1,0:T(8,128)(2,1)S(1)}, bf16[1024,2048]{1,0:T(8,128)(2,1)}, u32[]{:S(2)}) copy-start(bf16[1024,2048]{1,0:T(8,128)(2,1)} %param.5) | copy-start | bytes 12582916
  20.8 12.1 %copy-start.2 = (bf16[1024,2048]{1,0:T(8,128)(2,1)S(1)}, bf16[1024,2048]{1,0:T(8,128)(2,1)}, u32[]{:S(2)}) copy-start(bf16[1024,2048]{1,0:T(8,128)(2,1)} %param.5) | copy-start | bytes 12582916
  20.8 12.1 %copy-start.7 = (bf16[2048,128]{1,0:T(8,128)(2,1)S(1)}, bf16[2048,128]{1,0:T(8,128)(2,1)}, u32[]{:S(2)}) copy-start(bf16[2048,128]{1,0:T(8,128)(2,1)} %param.6) | copy-start | bytes 1572868
  26.6 28.5 %collective-permute-start = (bf16[1,8,273,128]{3,1,2,0:T(8,128)(2,1)}, bf16[1,8,273,128]{3,1,2,0:T(8,128)(2,1)}, u32[]{:S(2)}, u32[]{:S(2)}) collective-permute-start(bf16[1,8,273,128]{3,1,2,0:T(8,128)(2,1)} %copy.8), channel_id=1, source_target_pairs={{0,2},{2,4},{4,6},{6,0},{1,3},{3,5},{5,7},{7,1},{8,10},{10,12},{12... | collective-permute-start | bytes 1677320 | tf_op jit(solution)/shard_map/ppermute | solution.py:19
  29.6 27.1 %collective-permute-start.1 = (bf16[1,8,273,128]{3,1,2,0:T(8,128)(2,1)}, bf16[1,8,273,128]{3,1,2,0:T(8,128)(2,1)}, u32[]{:S(2)}, u32[]{:S(2)}) collective-permute-start(bf16[1,8,273,128]{3,1,2,0:T(8,128)(2,1)} %copy.8), channel_id=1, source_target_pairs={{0,6},{2,0},{4,2},{6,4},{1,7},{3,1},{5,3},{7,5},{8,14},{10,8},{12,... | collective-permute-start | bytes 1677320 | tf_op jit(solution)/shard_map/ppermute | solution.py:24
  34.5 0.7 copy-start.4
  50.6 4.4 %copy-start.5 = (bf16[1024,128]{0,1:T(8,128)(2,1)S(1)}, bf16[1024,128]{0,1:T(8,128)(2,1)}, u32[]{:S(2)}) copy-start(bf16[1024,128]{0,1:T(8,128)(2,1)} %copy-done.4) | copy-start | bytes 786436
  55.1 16.5 %collective-permute-start.2 = (bf16[1,8,273,128]{3,1,2,0:T(8,128)(2,1)}, bf16[1,8,273,128]{3,1,2,0:T(8,128)(2,1)}, u32[]{:S(2)}, u32[]{:S(2)}) collective-permute-start(bf16[1,8,273,128]{3,1,2,0:T(8,128)(2,1)} %collective-permute-done), channel_id=1, source_target_pairs={{0,2},{2,4},{4,6},{6,0},{1,3},{3,5},{5,7},{7,1},{8,10},{10,12},{12... | collective-permute-start | bytes 1677320 | tf_op jit(solution)/shard_map/ppermute | solution.py:19
  55.4 17.9 %copy-start.3 = (f32[8,128,1024]{2,1,0:T(8,128)S(1)}, f32[8,128,1024]{2,1,0:T(8,128)}, u32[]{:S(2)}) copy-start(f32[8,128,1024]{2,1,0:T(8,128)} %fusion) | copy-start | bytes 12582916
Sparse Core Ops, SparseCore 0:
  86.2 11.8 all-gather.1
